TPU v7x, 512 devices: a whole 4x8x8 slice. The times are simulated.
512 devices in a mesh: sub: 128 (over y, z, core), split: 4 (over x).
Axes of the slice: x: 4, y: 8, z: 8, core: 2. Of those that a mesh axis runs over, the one named last changes fastest.
Arguments:
- inv_conductance: float32 [128, 2048, 2048], P('sub', None, 'split')
- source_amp: float32 [128, 2048], P('sub', 'split'), may hold values from -6 to 6
- source_phase: float32 [128, 2048], P('sub', 'split'), may hold values from -3.140625 to 3.140625
- companion: float32 [128, 2048], P('sub', 'split'), may hold values from 0.1 to 0.8
- surge_impedance: float32 [128, 512], P('sub', 'split'), may hold values from 2 to 8
- initial_voltage: float32 [128, 64, 2048], P('sub', None, 'split'), may hold values from -6 to 6
- initial_history: float32 [128, 64, 512], P('sub', None, 'split'), may hold values from -6 to 6
- partner_sub: int32 [128, 512], P('sub', 'split'), may hold values from 0 to 127, as said below
- line_delay: int32 [128, 512], P('sub', 'split'), may hold values from 2 to 5, as said below
- open_step: int32 [128, 64, 512], P('sub', None, 'split'), may hold values from 0 to 15
Outputs:
- voltage: float32 [128, 64, 2048], P('sub', None, 'split')
- port_current: float32 [128, 64, 512], P('sub', None, 'split')
Inputs may be any that keep to these rules, and one draw needn't show every extreme that they name: partner_sub[partner_sub[s, p], p] == s and partner_sub[s, p] != s: a line joins port p of two subnetworks, both in the same block of 128 ports. At most 2 ports of one block of a subnetwork have lines to the same other subnetwork, and in every block some subnetwork gets exactly 2. `line_delay`: both ends of a line have the same delay.
All inputs are finite; a program needn't handle non-finite values.
Results may differ from a plain program's by a relative error of at most 0.00015.
Values sent between devices are 32-bit elements; how exact they have to be, the bound alone decides.
No kernel may reach another device: no remote copies, remote signals or barrier semaphores. Data moves between devices by JAX's collectives and lax.ppermute only.
A program may use at most 64 MiB of HBM per device.

v0:
```python
import jax
import jax.numpy as jnp
from jax import lax
from jax.experimental import pallas as pl
from jax.experimental.pallas import tpu as pltpu
from jax.sharding import PartitionSpec as P

STEPS = 8
DMIN = 2
DMAX = 5
STRIDE = 4
PARTS = 4

angular = 0.7

F32 = jnp.float32
BF16 = jnp.bfloat16
NT = (((1,), (1,)), ((), ()))
NN = (((1,), (0,)), ((), ()))
TN = (((0,), (0,)), ((), ()))


def two_pieces(array):
    high = array.astype(BF16)
    return high, (array - high.astype(F32)).astype(BF16)


def exact_dot(array, onehot, dims, array_first=True):
    high = array.astype(BF16)
    rest = array - high.astype(F32)
    middle = rest.astype(BF16)
    low = (rest - middle.astype(F32)).astype(BF16)
    total = None
    for piece in (high, middle, low):
        pair = (piece, onehot) if array_first else (onehot, piece)
        term = lax.dot_general(*pair, dims, preferred_element_type=F32)
        total = term if total is None else total + term
    return total


def iota(shape, dim):
    return lax.broadcasted_iota(jnp.int32, shape, dim)


def first_body(matrix, amp, phase, comp, volt, hist, delay, opens, out, table, stacked):
    cont, nodes = volt.shape
    ports = nodes // STRIDE

    @pl.when(pl.program_id(0) == 0)
    def _():
        times = (iota((STEPS, nodes), 0) + 1).astype(F32)
        source = amp[...] * jnp.cos(angular * times + phase[...])
        table[0:STEPS] = source
        table[STEPS:] = jnp.broadcast_to(comp[...], (STEPS, nodes))
        start = jnp.where(0 < delay[...], hist[...], 0.0)
        inject = jnp.where(0 < opens[...], start, 0.0)
        place = (iota((ports, nodes), 1) == STRIDE * iota((ports, nodes), 0)).astype(F32).astype(BF16)
        right = source[0:1] + comp[...] * volt[...] - exact_dot(inject, place, NN)
        high, low = two_pieces(right)
        stacked[:cont] = high
        stacked[cont:] = low

    high, low = two_pieces(matrix[...])
    both = lax.dot_general(stacked[...], high, NT, preferred_element_type=F32)
    rest = lax.dot_general(stacked[:cont], low, NT, preferred_element_type=F32)
    out[0] = both[:cont] + both[cont:] + rest


def prepare_body(matrix, table, order, high_out, low_out, table_out):
    nodes = matrix.shape[1]
    ports = nodes // STRIDE
    new = iota((nodes, nodes), 0)
    old = STRIDE * (new % ports) + new // ports
    moved = (iota((nodes, nodes), 1) == old).astype(F32).astype(BF16)
    order[...] = moved
    table_out[...] = exact_dot(table[...], moved, NT)
    for part in range(PARTS):
        pieces = two_pieces(matrix[part * nodes : (part + 1) * nodes])
        for piece, piece_out in zip(pieces, (high_out, low_out)):
            inputs = lax.dot_general(moved, piece, NT, preferred_element_type=F32).astype(BF16)
            piece_out[part] = lax.dot_general(inputs, moved, NT, preferred_element_type=F32).astype(BF16)


def history_at(step, start, delay, far):
    history = jnp.where(step < delay, start, 0.0)
    for anchor, array in far:
        history = jnp.where(delay == step - anchor, -array, history)
    return history


def step_body(step, anchors, high, low, table, volt, start, delay, opens, *refs):
    far = [(anchor, ref[...]) for anchor, ref in zip(anchors, refs)]
    out, kept = refs[len(anchors) :]
    cont, nodes = volt.shape
    ports = nodes // STRIDE
    history = history_at(step, start[...], delay[...], far)
    kept[...] = history
    right = table[step : step + 1] + table[STEPS : STEPS + 1] * volt[...]
    inject = jnp.where(step < opens[...], history, 0.0)
    right = jnp.concatenate([right[:, :ports] - inject, right[:, ports:]], 1)
    right_high, right_low = two_pieces(right)
    stacked = jnp.concatenate([right_high, right_low], 0)
    for part in range(PARTS):
        both = jnp.dot(stacked, high[part], preferred_element_type=F32)
        rest = jnp.dot(right_high, low[part], preferred_element_type=F32)
        out[part] = both[:cont] + both[cont:] + rest


def total_of(partial):
    total = partial[0]
    for part in range(1, PARTS):
        total = total + partial[part]
    return total


def close_body(step, partial, impedance, history, opens, *refs):
    volt, outgoing = refs[-2:]
    total = total_of(partial)
    if step == 0:
        total = exact_dot(total, refs[0][...], NT)
    volt[...] = total
    ports = impedance.shape[1]
    value = 2.0 * total[:, :ports] / impedance[...] + history[...]
    outgoing[...] = jnp.where(step < opens[...], value, 0.0)


def route_body(step, partial, impedance, history, opens, target, before, volt, buffer):
    total = total_of(partial)
    volt[...] = total
    slots = buffer.shape[0]
    ports = impedance.shape[1]
    value = 2.0 * total[:, :ports] / impedance[...] + history[...]
    outgoing = jnp.where(step < opens[...], value, 0.0)
    both = jnp.concatenate([before[...], outgoing], 0)
    routing = (iota((slots, ports), 0) == target[...]).astype(F32).astype(BF16)
    buffer[...] = exact_dot(both, routing, NT, array_first=False)


def unroute_body(buffer, target, first, second):
    slots = buffer.shape[0]
    cont, ports = first.shape
    routing = (iota((slots, ports), 0) == target[...]).astype(F32).astype(BF16)
    both = exact_dot(buffer[...], routing, TN)
    first[...] = both[:cont]
    second[...] = both[cont:]


def last_body(step, partial, impedance, history, opens, order, volt, current):
    total = total_of(partial)
    ports = impedance.shape[1]
    value = total[:, :ports] / impedance[...] + history[...]
    current[...] = jnp.where(step < opens[...], value, 0.0)
    volt[...] = exact_dot(total, order[...], NN)


def call(body, shapes, *arrays, name):
    whole = pl.BlockSpec(memory_space=pltpu.VMEM)
    return pl.pallas_call(
        body,
        in_specs=[whole] * len(arrays),
        out_specs=[whole] * len(shapes),
        out_shape=[jax.ShapeDtypeStruct(shape, kind) for shape, kind in shapes],
        compiler_params=pltpu.CompilerParams(vmem_limit_bytes=40 << 20),
        name=name,
    )(*arrays)


def local(
    inv_conductance,
    source_amp,
    source_phase,
    companion,
    surge_impedance,
    initial_voltage,
    initial_history,
    partner_sub,
    line_delay,
    open_step,
):
    matrix = inv_conductance[0]
    n_subs = lax.axis_size("sub")
    cont, nodes = initial_voltage.shape[1:]
    ports = initial_history.shape[2]
    capacity = max(2, 2 * ports // n_subs)
    slots = n_subs * capacity
    start = initial_history[0]
    opens = open_step[0]
    delay = line_delay
    impedance = surge_impedance

    small = lambda shape: pl.BlockSpec(shape, lambda part: (0, 0))
    partial, table = pl.pallas_call(
        first_body,
        grid=(PARTS,),
        in_specs=[
            pl.BlockSpec((nodes, nodes), lambda part: (part, 0)),
            small((1, nodes)),
            small((1, nodes)),
            small((1, nodes)),
            small((cont, nodes)),
            small((cont, ports)),
            small((1, ports)),
            small((cont, ports)),
        ],
        out_specs=[
            pl.BlockSpec((1, cont, nodes), lambda part: (part, 0, 0)),
            small((2 * STEPS, nodes)),
        ],
        out_shape=[
            jax.ShapeDtypeStruct((PARTS, cont, nodes), F32),
            jax.ShapeDtypeStruct((2 * STEPS, nodes), F32),
        ],
        scratch_shapes=[pltpu.VMEM((2 * cont, nodes), BF16)],
        name="first_step",
    )(matrix, source_amp, source_phase, companion, initial_voltage[0], start, delay, opens)

    order, high, low, table = call(
        prepare_body,
        [
            ((nodes, nodes), BF16),
            ((PARTS, nodes, nodes), BF16),
            ((PARTS, nodes, nodes), BF16),
            ((2 * STEPS, nodes), F32),
        ],
        matrix,
        table,
        name="prepare",
    )
    partner = partner_sub[0]
    position = jnp.arange(ports, dtype=jnp.int32)
    same_far = partner[:, None] == partner[None, :]
    earlier = position[:, None] > position[None, :]
    slot_rank = jnp.sum((same_far & earlier).astype(jnp.int32), axis=1)
    target = (partner * capacity + slot_rank)[None, :]

    history = start
    far = []
    before = None
    for step in range(STEPS):
        if step > 0:
            anchors = [a for a in range(len(far)) if DMIN <= step - a <= DMAX]
            partial, history = call(
                lambda *refs, step=step, anchors=anchors: step_body(step, anchors, *refs),
                [((PARTS, cont, nodes), F32), ((cont, ports), F32)],
                high,
                low,
                table,
                volt,
                start,
                delay,
                opens,
                *[far[a] for a in anchors],
                name=f"step_{step}",
            )
        arrived = lax.all_to_all(partial, "split", split_axis=0, concat_axis=0, tiled=True)
        if step == STEPS - 1:
            volt, current = call(
                lambda *refs, step=step: last_body(step, *refs),
                [((cont, nodes), F32), ((cont, ports), F32)],
                arrived,
                impedance,
                history,
                opens,
                order,
                name="last",
            )
        elif step + DMIN < STEPS and step % 2 == 1:
            volt, buffer = call(
                lambda *refs, step=step: route_body(step, *refs),
                [((cont, nodes), F32), ((slots, 2 * cont), F32)],
                arrived,
                impedance,
                history,
                opens,
                target,
                before,
                name=f"route_{step}",
            )
            buffer = buffer.reshape(n_subs, capacity, 2 * cont)
            incoming = lax.all_to_all(buffer, "sub", split_axis=0, concat_axis=0, tiled=True)
            far += call(
                unroute_body,
                [((cont, ports), F32), ((cont, ports), F32)],
                incoming.reshape(slots, 2 * cont),
                target,
                name=f"unroute_{step}",
            )
        else:
            volt, before = call(
                lambda *refs, step=step: close_body(step, *refs),
                [((cont, nodes), F32), ((cont, ports), F32)],
                arrived,
                impedance,
                history,
                opens,
                *([order] if step == 0 else []),
                name=f"close_{step}",
            )
    return (volt[None], current[None])


def solution(mesh):
    placed = (
        P("sub", None, "split"),
        P("sub", "split"),
        P("sub", "split"),
        P("sub", "split"),
        P("sub", "split"),
        P("sub", None, "split"),
        P("sub", None, "split"),
        P("sub", "split"),
        P("sub", "split"),
        P("sub", None, "split"),
    )
    return jax.shard_map(
        local,
        mesh=mesh,
        in_specs=placed,
        out_specs=(P("sub", None, "split"), P("sub", None, "split")),
        check_vma=False,
    )
```

profile of v0, /device:TPU:16, one launch (start us, length us, event | category | flops | bytes accessed | tf_op | source)
XLA Modules:
  0.0 181.8 jit_solution(6558083482941849638)
XLA Ops:
  0.6 5.0 %first_step.1 = (f32[4,64,512]{2,1,0:T(8,128)}, f32[16,512]{1,0:T(8,128)}) custom-call(f32[2048,512]{1,0:T(8,128)} %bitcast.15, f32[1,512]{1,0:T(1,128)} %amp.1, f32[1,512]{1,0:T(1,128)} %phase.1, f32[1,512]{1,0:T(1,128)} %comp.1, f32[64,512]{1,0:T(8,128)} %bitcast.48, f32[64,128]{1,0:T(8,128)} %bitcast.33, s32[1,128]{1,0:T(1,128)} %refs_5_.13, ...), custom_call_target="tpu_custom_call" | custom-call | tf_op jit(solution)/shard_map/first_step/pallas_call | solution.py:192
  5.6 4.3 %all-to-all-start = ((f32[4,64,512]{2,1,0:T(8,128)}), f32[4,64,512]{2,1,0:T(8,128)S(1)}, u32[]{:S(2)}, u32[]{:S(2)}) async-start(f32[4,64,512]{2,1,0:T(8,128)} %get-tuple-element.47), calls=%async_computation | async-start | bytes 1048576 | tf_op jit(solution)/shard_map/all_to_all | solution.py:255
  9.9 2.2 %copy-done.4 = f32[1,2048,512]{2,1,0:T(8,128)S(1)} copy-done((f32[1,2048,512]{2,1,0:T(8,128)S(1)}, f32[1,2048,512]{2,1,0:T(8,128)}, u32[]{:S(2)}) %copy-start.4) | copy-done | bytes 4194328
  12.9 5.1 %prepare.1 = (bf16[512,512]{1,0:T(8,128)(2,1)S(1)}, bf16[4,512,512]{2,1,0:T(8,128)(2,1)S(1)}, bf16[4,512,512]{2,1,0:T(8,128)(2,1)S(1)}, f32[16,512]{1,0:T(8,128)S(1)}) custom-call(f32[2048,512]{1,0:T(8,128)S(1)} %bitcast.16, f32[16,512]{1,0:T(8,128)S(1)} %copy-done.8), custom_call_target="tpu_custom_call" | custom-call | tf_op jit(solution)/shard_map/prepare/pallas_call | solution.py:158
  18.0 1.3 copy-done
  20.0 1.6 copy-done.1
  23.2 4.8 %all-to-all-start.1 = ((f32[4,64,512]{2,1,0:T(8,128)}), f32[4,64,512]{2,1,0:T(8,128)S(1)}, u32[]{:S(2)}, u32[]{:S(2)}) async-start(f32[4,64,512]{2,1,0:T(8,128)} %copy-done.7), calls=%async_computation.1 | async-start | bytes 1048576 | tf_op jit(solution)/shard_map/all_to_all | solution.py:255
  28.2 8.7 %all-to-all-done.1.refs_0_ = f32[4,64,512]{2,1,0:T(8,128)S(1)} async-done(((f32[4,64,512]{2,1,0:T(8,128)}), f32[4,64,512]{2,1,0:T(8,128)S(1)}, u32[]{:S(2)}, u32[]{:S(2)}) %all-to-all-start.1) | async-done | bytes 524320 | tf_op jit(solution)/shard_map/all_to_all | solution.py:255
  37.2 28.4 %all_to_all.55 = f32[128,2,128]{2,1,0:T(2,128)S(1)} all-to-all(f32[128,2,128]{2,1,0:T(2,128)S(1)} %bitcast.45), channel_id=1, replica_groups=mesh['sub'=128,'split'=4] {'sub'}, dimensions={0} | all-to-all | bytes 262144 | tf_op jit(solution)/shard_map/all_to_all | solution.py:280
  65.8 1.6 copy-done.2
  68.2 12.4 %all_to_all.56.refs_0_ = f32[4,64,512]{2,1,0:T(8,128)S(1)} all-to-all(f32[4,64,512]{2,1,0:T(8,128)S(1)} %get-tuple-element.56), channel_id=1, replica_groups=mesh['sub'=128,'split'=4] {'split'}, dimensions={0} | all-to-all | bytes 1048576 | tf_op jit(solution)/shard_map/all_to_all | solution.py:255
  80.7 0.8 step_3.1
  81.5 11.6 %all_to_all.57.refs_0_ = f32[4,64,512]{2,1,0:T(8,128)S(1)} all-to-all(f32[4,64,512]{2,1,0:T(8,128)S(1)} %get-tuple-element.60), channel_id=1, replica_groups=mesh['sub'=128,'split'=4] {'split'}, dimensions={0} | all-to-all | bytes 1048576 | tf_op jit(solution)/shard_map/all_to_all | solution.py:255
  93.4 17.3 %all_to_all.58 = f32[128,2,128]{2,1,0:T(2,128)S(1)} all-to-all(f32[128,2,128]{2,1,0:T(2,128)S(1)} %bitcast.46), channel_id=1, replica_groups=mesh['sub'=128,'split'=4] {'sub'}, dimensions={0} | all-to-all | bytes 262144 | tf_op jit(solution)/shard_map/all_to_all | solution.py:280
  110.9 0.8 step_4.1
  111.7 12.4 %all_to_all.59.refs_0_ = f32[4,64,512]{2,1,0:T(8,128)S(1)} all-to-all(f32[4,64,512]{2,1,0:T(8,128)S(1)} %get-tuple-element.66), channel_id=1, replica_groups=mesh['sub'=128,'split'=4] {'split'}, dimensions={0} | all-to-all | bytes 1048576 | tf_op jit(solution)/shard_map/all_to_all | solution.py:255
  124.2 0.8 step_5.1
  125.0 11.6 %all_to_all.60.refs_0_ = f32[4,64,512]{2,1,0:T(8,128)S(1)} all-to-all(f32[4,64,512]{2,1,0:T(8,128)S(1)} %get-tuple-element.70), channel_id=1, replica_groups=mesh['sub'=128,'split'=4] {'split'}, dimensions={0} | all-to-all | bytes 1048576 | tf_op jit(solution)/shard_map/all_to_all | solution.py:255
  136.9 17.3 %all_to_all.61 = f32[128,2,128]{2,1,0:T(2,128)S(1)} all-to-all(f32[128,2,128]{2,1,0:T(2,128)S(1)} %bitcast.47), channel_id=1, replica_groups=mesh['sub'=128,'split'=4] {'sub'}, dimensions={0} | all-to-all | bytes 262144 | tf_op jit(solution)/shard_map/all_to_all | solution.py:280
  154.4 0.8 step_6.1
  155.3 12.4 %all_to_all.62.refs_0_ = f32[4,64,512]{2,1,0:T(8,128)S(1)} all-to-all(f32[4,64,512]{2,1,0:T(8,128)S(1)} %get-tuple-element.76), channel_id=1, replica_groups=mesh['sub'=128,'split'=4] {'split'}, dimensions={0} | all-to-all | bytes 1048576 | tf_op jit(solution)/shard_map/all_to_all | solution.py:255
  168.3 0.8 step_7.1
  169.2 11.6 %all_to_all.63.refs_0_ = f32[4,64,512]{2,1,0:T(8,128)S(1)} all-to-all(f32[4,64,512]{2,1,0:T(8,128)S(1)} %get-tuple-element.80), channel_id=1, replica_groups=mesh['sub'=128,'split'=4] {'split'}, dimensions={0} | all-to-all | bytes 1048576 | tf_op jit(solution)/shard_map/all_to_all | solution.py:255
  180.8 1.0 last.1
  (35 shorter events, 6.2 us)
Async XLA Ops:
  5.6 13.8 %all-to-all-start = ((f32[4,64,512]{2,1,0:T(8,128)}), f32[4,64,512]{2,1,0:T(8,128)S(1)}, u32[]{:S(2)}, u32[]{:S(2)}) async-start(f32[4,64,512]{2,1,0:T(8,128)} %get-tuple-element.47), calls=%async_computation | async-start | bytes 1048576 | tf_op jit(solution)/shard_map/all_to_all | solution.py:255
  9.9 2.2 %copy-start.4 = (f32[1,2048,512]{2,1,0:T(8,128)S(1)}, f32[1,2048,512]{2,1,0:T(8,128)}, u32[]{:S(2)}) copy-start(f32[1,2048,512]{2,1,0:T(8,128)} %param.10) | copy-start | bytes 12582916
  12.1 0.8 copy-start.8
  12.9 6.5 %copy-start.5 = (s32[1,64,128]{2,1,0:T(8,128)S(1)}, s32[1,64,128]{2,1,0:T(8,128)}, u32[]{:S(2)}) copy-start(s32[1,64,128]{2,1,0:T(8,128)} %param.19) | copy-start | bytes 98308
  12.9 6.5 %copy-start.6 = (f32[1,64,128]{2,1,0:T(8,128)S(1)}, f32[1,64,128]{2,1,0:T(8,128)}, u32[]{:S(2)}) copy-start(f32[1,64,128]{2,1,0:T(8,128)} %param.16) | copy-start | bytes 98308
  12.9 6.5 %copy-start.10 = (f32[1,128]{1,0:T(1,128)S(1)}, f32[1,128]{1,0:T(1,128)}, u32[]{:S(2)}) copy-start(f32[1,128]{1,0:T(1,128)} %refs_1_.15) | copy-start | bytes 1540
  12.9 7.1 %copy-start.9 = (s32[1,128]{1,0:T(1,128)S(1)}, s32[1,128]{1,0:T(1,128)}, u32[]{:S(2)}) copy-start(s32[1,128]{1,0:T(1,128)} %refs_5_.13) | copy-start | bytes 1540
  18.0 1.4 copy-start
  20.0 1.6 copy-start.1
  21.6 6.4 %copy-start.11 = (s32[1,128]{1,0:T(1,128)S(1)}, s32[1,128]{1,0:T(1,128)}, u32[]{:S(2)}) copy-start(s32[1,128]{1,0:T(1,128)} %param.17) | copy-start | bytes 1540
  22.4 0.8 copy-start.7
  23.2 13.7 %all-to-all-start.1 = ((f32[4,64,512]{2,1,0:T(8,128)}), f32[4,64,512]{2,1,0:T(8,128)S(1)}, u32[]{:S(2)}, u32[]{:S(2)}) async-start(f32[4,64,512]{2,1,0:T(8,128)} %copy-done.7), calls=%async_computation.1 | async-start | bytes 1048576 | tf_op jit(solution)/shard_map/all_to_all | solution.py:255
  65.8 1.6 copy-start.2
  67.4 13.3 %copy-start.3 = (bf16[4,512,512]{2,1,0:T(8,128)(2,1)S(1)}, bf16[4,512,512]{2,1,0:T(8,128)(2,1)}, u32[]{:S(2)}) copy-start(bf16[4,512,512]{2,1,0:T(8,128)(2,1)} %copy-done) | copy-start | bytes 6291460
where the time goes:
time: 183 us; the launch traced here: 182 us
  blocking collectives  135 us (74%)
  Pallas kernels  19.6 us (11%)
  starting transfers between devices  9.07 us (5%)
  waiting for transfers between devices  8.76 us (5%)
  local copies, waits for them, and re-layouts  8.28 us (5%)
    all_to_all x6, blocking collectives, local(): lax.all_to_all(partial, 'split', split_axis=0, concat_axis=0, tiled=True)  72.1 us
    all_to_all x3, blocking collectives, local(): lax.all_to_all(buffer, 'sub', split_axis=0, concat_axis=0, tiled=True)  62.9 us
    pallas_call x19, Pallas kernels, call(): pl.pallas_call(body, in_specs=[whole] * len(arrays), out_specs=[whole] *...  14.6 us
    all_to_all x2, starting transfers between devices, local(): lax.all_to_all(partial, 'split', split_axis=0, concat_axis=0, tiled=True)  9.07 us
    all_to_all x2, waiting for transfers between devices, local(): lax.all_to_all(partial, 'split', split_axis=0, concat_axis=0, tiled=True)  8.76 us
    unnamed x24, local copies, waits for them, and re-layouts  8.28 us
    pallas_call x1, Pallas kernels, local(): pl.pallas_call(first_body, grid=(PARTS,), in_specs=[pl.BlockSpec((nodes,...  5 us
  transfers between devices with their start and end apart: 2, of which 1 were waited for; matrix products, arithmetic and copies ran while one was open for 0% of the time, Pallas kernels for 3%

commit v1 on v0

v1 whole, which is shorter than its diff:
```python
import jax
import jax.numpy as jnp
from jax import lax
from jax.experimental import pallas as pl
from jax.experimental.pallas import tpu as pltpu
from jax.sharding import PartitionSpec as P

STEPS = 8
DMIN = 2
DMAX = 5
STRIDE = 4
PARTS = 4
NEAR = 1

angular = 0.7

F32 = jnp.float32
BF16 = jnp.bfloat16
NT = (((1,), (1,)), ((), ()))
NN = (((1,), (0,)), ((), ()))
TN = (((0,), (0,)), ((), ()))


def two_pieces(array):
    high = array.astype(BF16)
    return high, (array - high.astype(F32)).astype(BF16)


def exact_dot(array, onehot, dims, array_first=True):
    high = array.astype(BF16)
    rest = array - high.astype(F32)
    middle = rest.astype(BF16)
    low = (rest - middle.astype(F32)).astype(BF16)
    total = None
    for piece in (high, middle, low):
        pair = (piece, onehot) if array_first else (onehot, piece)
        term = lax.dot_general(*pair, dims, preferred_element_type=F32)
        total = term if total is None else total + term
    return total


def stacked_exact_dot(array, onehot, dims):
    rows = array.shape[0]
    high = array.astype(BF16)
    rest = array - high.astype(F32)
    middle = rest.astype(BF16)
    low = (rest - middle.astype(F32)).astype(BF16)
    pieces = jnp.concatenate([high, middle, low], 0)
    terms = lax.dot_general(pieces, onehot, dims, preferred_element_type=F32)
    return terms[:rows] + terms[rows : 2 * rows] + terms[2 * rows :]


def iota(shape, dim):
    return lax.broadcasted_iota(jnp.int32, shape, dim)


def start_strips(matrix, strips, sems, forward=True):
    copies = {}
    width = strips.shape[2]
    for part in range(PARTS) if forward else reversed(range(PARTS)):
        rows = pl.ds(part * strips.shape[1] // PARTS, strips.shape[1] // PARTS)
        for strip in range(strips.shape[0]):
            copies[part, strip] = pltpu.make_async_copy(
                matrix.at[rows, pl.ds(strip * width, width)],
                strips.at[strip, rows, :],
                sems.at[part, strip],
            )
            copies[part, strip].start()
    return copies


def part_rows(strips, copies, part):
    count, rows, width = strips.shape
    nodes = rows // PARTS
    ports = nodes // STRIDE
    columns = []
    for strip in range(count):
        copies[part, strip].wait()
        pieces = [
            strips[strip, pl.ds(part * nodes + lane, ports, stride=STRIDE), :] for lane in range(STRIDE)
        ]
        columns.append(jnp.concatenate(pieces, 0))
    return jnp.concatenate(columns, 1)


def product(stacked, cont, high, low, dims):
    both = lax.dot_general(stacked, high, dims, preferred_element_type=F32)
    rest = lax.dot_general(stacked[:cont], low, dims, preferred_element_type=F32)
    return both[:cont] + both[cont:] + rest


def first_body(*refs):
    ins, (matrix, table, out, *held, small_sems, strips, sems, block, sent) = refs[:7], refs[7:]
    fetches = [pltpu.make_async_copy(a, b, small_sems.at[n]) for n, (a, b) in enumerate(zip(ins, held))]
    for copy in fetches:
        copy.start()
    copies = start_strips(matrix, strips, sems)
    for copy in fetches:
        copy.wait()
    amp, phase, comp, volt, start, delay, opens = held
    cont, nodes = volt.shape
    ports = nodes // STRIDE
    times = (iota((STEPS, nodes), 0) + 1).astype(F32)
    source = amp[...] * jnp.cos(angular * times + phase[...])
    table[0:STEPS] = source
    table[STEPS:] = jnp.broadcast_to(comp[...], (STEPS, nodes))
    history = jnp.where(0 < delay[...], start[...], 0.0)
    inject = jnp.where(0 < opens[...], history, 0.0)
    place = (iota((ports, nodes), 1) == STRIDE * iota((ports, nodes), 0)).astype(F32).astype(BF16)
    right = source[0:1] + comp[...] * volt[...] - stacked_exact_dot(inject, place, NN)
    stacked = jnp.concatenate(two_pieces(right), 0)
    leaving = []
    for part in range(PARTS):
        high, low = two_pieces(part_rows(strips, copies, part))
        block[part] = product(stacked, cont, high, low, NT)
        leaving.append(pltpu.make_async_copy(block.at[part], out.at[part], sent.at[part]))
        leaving[-1].start()
    for copy in leaving:
        copy.wait()


def prepare_body(
    capacity, table, partner, matrix, low_out, high_near, table_out, target, order_out, high_far, strips, sems, high, order, sent
):
    copies = start_strips(matrix, strips, sems, forward=False)
    nodes = table.shape[1]
    ports = nodes // STRIDE
    new = iota((nodes, nodes), 0)
    old = STRIDE * (new % ports) + new // ports
    moved = (iota((nodes, nodes), 1) == old).astype(F32).astype(BF16)
    order[...] = moved
    leaving = [pltpu.make_async_copy(order, order_out, sent.at[PARTS - NEAR])]
    leaving[-1].start()
    table_out[...] = stacked_exact_dot(table[...], moved, NT)
    across = jnp.broadcast_to(partner[...].astype(F32), (ports, ports))
    earlier = (across == across.T) & (iota((ports, ports), 0) < iota((ports, ports), 1))
    rank = jnp.sum(earlier.astype(F32), axis=0, keepdims=True).astype(jnp.int32)
    target[...] = partner[...] * capacity + rank
    for part in reversed(range(PARTS)):
        pieces = two_pieces(part_rows(strips, copies, part))
        terms = [lax.dot_general(moved, piece, NT, preferred_element_type=F32).astype(BF16) for piece in pieces]
        low_out[part] = terms[1]
        if part < NEAR:
            high_near[part] = terms[0]
        else:
            far = part - NEAR
            high[far] = terms[0]
            leaving.append(pltpu.make_async_copy(high.at[far], high_far.at[far], sent.at[far]))
            leaving[-1].start()
    for copy in leaving:
        copy.wait()


def history_at(step, start, delay, far):
    history = jnp.where(step < delay, start, 0.0)
    for anchor, array in far:
        history = jnp.where(delay == step - anchor, -array, history)
    return history


def total_of(partial):
    total = partial[0]
    for part in range(1, PARTS):
        total = total + partial[part]
    return total


def outgoing_of(step, total, impedance, history, opens):
    ports = impedance.shape[1]
    value = 2.0 * total[:, :ports] / impedance[...] + history
    return jnp.where(step < opens[...], value, 0.0)


def onehot_of(target, slots):
    return (iota((slots, target.shape[1]), 0) == target[...]).astype(F32).astype(BF16)


def multiply(step, volt, history, highs, low, table, opens, out):
    cont, nodes = volt.shape
    ports = nodes // STRIDE
    right = table[step : step + 1] + table[STEPS : STEPS + 1] * volt
    inject = jnp.where(step < opens[...], history, 0.0)
    right = jnp.concatenate([right[:, :ports] - inject, right[:, ports:]], 1)
    stacked = jnp.concatenate(two_pieces(right), 0)
    for part in range(PARTS):
        high = highs[0][part] if part < NEAR else highs[1][part - NEAR]
        out[part] = product(stacked, cont, high, low[part], NN)


def odd_body(step, anchors, near, high, low, table, start, delay, opens, impedance, history, partial, *refs):
    far = [(anchor, ref[...]) for anchor, ref in zip(anchors, refs)]
    out, kept, *outgoing = refs[len(anchors) :]
    total = total_of(partial)
    for ref in outgoing:
        ref[...] = outgoing_of(step - 1, total, impedance, history[...], opens)
    now = history_at(step, start[...], delay[...], far)
    kept[...] = now
    multiply(step, total, now, (near, high), low, table, opens, out)


def even_body(step, anchors, near, high, low, table, start, delay, opens, target, volt, buffer, *refs):
    out, kept, *newest = refs[len(anchors) :]
    cont, ports = start.shape
    both = exact_dot(buffer[...], onehot_of(target, buffer.shape[0]), TN)
    latest = [both[:cont], both[cont:]]
    for ref, array in zip(newest, latest):
        ref[...] = array
    far = [(anchor, ref[...]) for anchor, ref in zip(anchors, refs)] + [(step - DMIN, latest[0])]
    now = history_at(step, start[...], delay[...], far)
    kept[...] = now
    multiply(step, volt[...], now, (near, high), low, table, opens, out)


def route_body(step, partial, impedance, history, opens, target, before, volt, buffer):
    total = total_of(partial)
    volt[...] = total
    outgoing = outgoing_of(step, total, impedance, history[...], opens)
    both = jnp.concatenate([before[...], outgoing], 0)
    buffer[...] = exact_dot(both, onehot_of(target, buffer.shape[0]), NT, array_first=False)


def last_body(step, partial, impedance, history, opens, order, volt, current):
    total = total_of(partial)
    ports = impedance.shape[1]
    value = total[:, :ports] / impedance[...] + history[...]
    current[...] = jnp.where(step < opens[...], value, 0.0)
    volt[...] = stacked_exact_dot(total, order[...], NN)


def call(body, shapes, *arrays, name, far_in=(), far_out=(), scratch=()):
    whole = pl.BlockSpec(memory_space=pltpu.VMEM)
    away = pl.BlockSpec(memory_space=pltpu.HBM)
    return pl.pallas_call(
        body,
        in_specs=[whole] * len(arrays) + [away] * len(far_in),
        out_specs=[whole] * len(shapes) + [away] * len(far_out),
        out_shape=[jax.ShapeDtypeStruct(*shape) for shape in shapes] + [pltpu.HBM(*shape) for shape in far_out],
        scratch_shapes=list(scratch),
        compiler_params=pltpu.CompilerParams(vmem_limit_bytes=40 << 20),
        name=name,
    )(*arrays, *[pltpu.with_memory_space_constraint(array, pltpu.HBM) for array in far_in])


def local(
    inv_conductance,
    source_amp,
    source_phase,
    companion,
    surge_impedance,
    initial_voltage,
    initial_history,
    partner_sub,
    line_delay,
    open_step,
):
    matrix = inv_conductance[0]
    n_subs = lax.axis_size("sub")
    cont, nodes = initial_voltage.shape[1:]
    ports = initial_history.shape[2]
    capacity = max(2, 2 * ports // n_subs)
    slots = n_subs * capacity
    start = initial_history[0]
    opens = open_step[0]
    delay = line_delay
    impedance = surge_impedance
    port_shape = ((cont, ports), F32)
    split_shape = ((PARTS, cont, nodes), F32)

    order_shape = ((nodes, nodes), BF16)
    far_matrix = ((PARTS - NEAR, nodes, nodes), BF16)
    strips = [pltpu.VMEM((STRIDE, PARTS * nodes, ports), F32), pltpu.SemaphoreType.DMA((PARTS, STRIDE))]

    inputs = [source_amp, source_phase, companion, initial_voltage[0], start, delay, opens]
    table, partial = call(
        first_body,
        [((2 * STEPS, nodes), F32)],
        far_in=[*inputs, matrix],
        far_out=[split_shape],
        scratch=[
            *[pltpu.VMEM(array.shape, array.dtype) for array in inputs],
            pltpu.SemaphoreType.DMA((len(inputs),)),
            *strips,
            pltpu.VMEM(*split_shape),
            pltpu.SemaphoreType.DMA((PARTS,)),
        ],
        name="first_step",
    )
    low, near, table, target, order, high = call(
        lambda *refs: prepare_body(capacity, *refs),
        [
            ((PARTS, nodes, nodes), BF16),
            ((NEAR, nodes, nodes), BF16),
            ((2 * STEPS, nodes), F32),
            ((1, ports), jnp.int32),
        ],
        table,
        partner_sub,
        far_in=[matrix],
        far_out=[order_shape, far_matrix],
        scratch=[*strips, pltpu.VMEM(*far_matrix), pltpu.VMEM(*order_shape), pltpu.SemaphoreType.DMA((PARTS - NEAR + 1,))],
        name="prepare",
    )

    history = start
    far = []
    for step in range(STEPS):
        anchors = [a for a in range(step) if DMIN <= step - a <= DMAX]
        if step % 2 == 1:
            partial, history, *before = call(
                lambda *refs, step=step, anchors=anchors: odd_body(step, anchors, *refs),
                [split_shape, port_shape] + [port_shape] * (step + DMIN < STEPS),
                near,
                high,
                low,
                table,
                start,
                delay,
                opens,
                impedance,
                history,
                arrived,
                *[far[a] for a in anchors],
                name=f"step_{step}",
            )
        elif step > 0:
            anchors = anchors[:-1]
            partial, history, *newest = call(
                lambda *refs, step=step, anchors=anchors: even_body(step, anchors, *refs),
                [split_shape] + [port_shape] * 3,
                near,
                high,
                low,
                table,
                start,
                delay,
                opens,
                target,
                volt,
                incoming.reshape(slots, 2 * cont),
                *[far[a] for a in anchors],
                name=f"step_{step}",
            )
            far += newest
        arrived = lax.all_to_all(partial, "split", split_axis=0, concat_axis=0, tiled=True)
        if step == STEPS - 1:
            volt, current = call(
                lambda *refs, step=step: last_body(step, *refs),
                [((cont, nodes), F32), port_shape],
                arrived,
                impedance,
                history,
                opens,
                order,
                name="last",
            )
        elif step % 2 == 1:
            volt, buffer = call(
                lambda *refs, step=step: route_body(step, *refs),
                [((cont, nodes), F32), ((slots, 2 * cont), F32)],
                arrived,
                impedance,
                history,
                opens,
                target,
                *before,
                name=f"route_{step}",
            )
            buffer = buffer.reshape(n_subs, capacity, 2 * cont)
            incoming = lax.all_to_all(buffer, "sub", split_axis=0, concat_axis=0, tiled=True)
    return (volt[None], current[None])


def solution(mesh):
    placed = (
        P("sub", None, "split"),
        P("sub", "split"),
        P("sub", "split"),
        P("sub", "split"),
        P("sub", "split"),
        P("sub", None, "split"),
        P("sub", None, "split"),
        P("sub", "split"),
        P("sub", "split"),
        P("sub", None, "split"),
    )
    return jax.shard_map(
        local,
        mesh=mesh,
        in_specs=placed,
        out_specs=(P("sub", None, "split"), P("sub", None, "split")),
        check_vma=False,
    )
```

time: 183 us -> 176 us (0.962)
  blocking collectives: 135 us -> 146 us
  local copies, waits for them, and re-layouts: 8.28 us -> 1.43 us
  starting transfers between devices: 9.07 us -> 4.3 us
  waiting for transfers between devices: 8.76 us -> 4.61 us
    all_to_all x6 -> x7, blocking collectives: 72.1 us -> 82.9 us  [local(): lax.all_to_all(partial, 'split', split_axis=0, concat_axis=0, tiled=True)]
    unnamed x24 -> x16, local copies, waits for them, and re-layouts: 8.28 us -> 1.43 us
    all_to_all x2 -> x1, starting transfers between devices: 9.07 us -> 4.3 us  [local(): lax.all_to_all(partial, 'split', split_axis=0, concat_axis=0, tiled=True)]
    all_to_all x2 -> x1, waiting for transfers between devices: 8.76 us -> 4.61 us  [local(): lax.all_to_all(partial, 'split', split_axis=0, concat_axis=0, tiled=True)]
    pallas_call x20 -> x13, Pallas kernels: 19.6 us -> 18 us  [call(): pl.pallas_call(body, in_specs=[whole] * len(arrays) + [away] * len(far_in...]
  transfers between devices with their start and end apart: 2 -> 1, of which waited for: 1 -> 1; matrix products, arithmetic and copies ran while one was open for 0% -> 0% of each run, Pallas kernels for 3% -> 3%
where the time goes in v1:
time: 176 us; the launch traced here: 175 us
  blocking collectives  146 us (83%)
  Pallas kernels  18 us (10%)
  waiting for transfers between devices  4.61 us (3%)
  starting transfers between devices  4.3 us (2%)
    all_to_all x7, blocking collectives, local(): lax.all_to_all(partial, 'split', split_axis=0, concat_axis=0, tiled=True)  82.9 us
    all_to_all x3, blocking collectives, local(): lax.all_to_all(buffer, 'sub', split_axis=0, concat_axis=0, tiled=True)  62.9 us
    pallas_call x13, Pallas kernels, call(): pl.pallas_call(body, in_specs=[whole] * len(arrays) + [away] * len(far_in...  18 us
    all_to_all x1, waiting for transfers between devices, local(): lax.all_to_all(partial, 'split', split_axis=0, concat_axis=0, tiled=True)  4.61 us
    all_to_all x1, starting transfers between devices, local(): lax.all_to_all(partial, 'split', split_axis=0, concat_axis=0, tiled=True)  4.3 us
  transfers between devices with their start and end apart: 1, of which 1 were waited for; matrix products, arithmetic and copies ran while one was open for 0% of the time, Pallas kernels for 3%

profile of v1, /device:TPU:16, one launch (start us, length us, event | category | flops | bytes accessed | tf_op | source)
XLA Modules:
  0.0 175.0 jit_solution(7012346211903255469)
XLA Ops:
  0.6 5.2 %first_step.1 = (f32[16,512]{1,0:T(8,128)S(1)}, f32[4,64,512]{2,1,0:T(8,128)}) custom-call(f32[1,512]{1,0:T(1,128)} %refs_0_.1, f32[1,512]{1,0:T(1,128)} %refs_1_.6, f32[1,512]{1,0:T(1,128)} %refs_2_.1, f32[64,512]{1,0:T(8,128)} %bitcast.41, f32[64,128]{1,0:T(8,128)} %bitcast.24, s32[1,128]{1,0:T(1,128)} %refs_5_.15, s32[64,128]{1,0:T(8,128)} %bitcast.12, ...), custom_call_target="tpu_custom_call" | custom-call | tf_op jit(solution)/shard_map/first_step/pallas_call | solution.py:233
  5.9 4.3 %all-to-all-start = ((f32[4,64,512]{2,1,0:T(8,128)}), f32[4,64,512]{2,1,0:T(8,128)S(1)}, u32[]{:S(2)}, u32[]{:S(2)}) async-start(f32[4,64,512]{2,1,0:T(8,128)} %get-tuple-element.47), calls=%async_computation | async-start | bytes 1048576 | tf_op jit(solution)/shard_map/all_to_all | solution.py:344
  10.2 4.8 %prepare.1 = (bf16[4,512,512]{2,1,0:T(8,128)(2,1)S(1)}, bf16[1,512,512]{2,1,0:T(8,128)(2,1)S(1)}, f32[16,512]{1,0:T(8,128)S(1)}, s32[1,128]{1,0:T(1,128)S(1)}, b...) custom-call(f32[16,512]{1,0:T(8,128)S(1)} %get-tuple-element.41.refs_0_, s32[1,128]{1,0:T(1,128)S(1)} %copy-done.7, ...), custom_call_target="tpu_custom_call" | custom-call | tf_op jit(solution)/shard_map/prepare/pallas_call | solution.py:233
  15.0 4.6 %all-to-all-done.refs_9_ = f32[4,64,512]{2,1,0:T(8,128)S(1)} async-done(((f32[4,64,512]{2,1,0:T(8,128)}), f32[4,64,512]{2,1,0:T(8,128)S(1)}, u32[]{:S(2)}, u32[]{:S(2)}) %all-to-all-start) | async-done | bytes 524320 | tf_op jit(solution)/shard_map/all_to_all | solution.py:344
  19.7 1.4 copy-done
  21.1 0.8 step_1.1
  21.9 10.8 %all_to_all.55.refs_0_ = f32[4,64,512]{2,1,0:T(8,128)S(1)} all-to-all(f32[4,64,512]{2,1,0:T(8,128)S(1)} %get-tuple-element.48), channel_id=1, replica_groups=mesh['sub'=128,'split'=4] {'split'}, dimensions={0} | all-to-all | bytes 1048576 | tf_op jit(solution)/shard_map/all_to_all | solution.py:344
  32.7 0.2 route_1.1
  33.0 28.4 %all_to_all.56 = f32[128,2,128]{2,1,0:T(2,128)S(1)} all-to-all(f32[128,2,128]{2,1,0:T(2,128)S(1)} %bitcast.36), channel_id=1, replica_groups=mesh['sub'=128,'split'=4] {'sub'}, dimensions={0} | all-to-all | bytes 262144 | tf_op jit(solution)/shard_map/all_to_all | solution.py:369
  61.3 1.0 step_2.1
  62.3 12.4 %all_to_all.57.refs_9_ = f32[4,64,512]{2,1,0:T(8,128)S(1)} all-to-all(f32[4,64,512]{2,1,0:T(8,128)S(1)} %get-tuple-element.54), channel_id=1, replica_groups=mesh['sub'=128,'split'=4] {'split'}, dimensions={0} | all-to-all | bytes 1048576 | tf_op jit(solution)/shard_map/all_to_all | solution.py:344
  74.8 0.8 step_3.1
  75.6 11.6 %all_to_all.58.refs_0_ = f32[4,64,512]{2,1,0:T(8,128)S(1)} all-to-all(f32[4,64,512]{2,1,0:T(8,128)S(1)} %get-tuple-element.57), channel_id=1, replica_groups=mesh['sub'=128,'split'=4] {'split'}, dimensions={0} | all-to-all | bytes 1048576 | tf_op jit(solution)/shard_map/all_to_all | solution.py:344
  87.5 17.3 %all_to_all.59 = f32[128,2,128]{2,1,0:T(2,128)S(1)} all-to-all(f32[128,2,128]{2,1,0:T(2,128)S(1)} %bitcast.37), channel_id=1, replica_groups=mesh['sub'=128,'split'=4] {'sub'}, dimensions={0} | all-to-all | bytes 262144 | tf_op jit(solution)/shard_map/all_to_all | solution.py:369
  104.7 1.0 step_4.1
  105.8 12.4 %all_to_all.60.refs_9_ = f32[4,64,512]{2,1,0:T(8,128)S(1)} all-to-all(f32[4,64,512]{2,1,0:T(8,128)S(1)} %get-tuple-element.63), channel_id=1, replica_groups=mesh['sub'=128,'split'=4] {'split'}, dimensions={0} | all-to-all | bytes 1048576 | tf_op jit(solution)/shard_map/all_to_all | solution.py:344
  118.2 0.8 step_5.1
  119.0 11.6 %all_to_all.61.refs_0_ = f32[4,64,512]{2,1,0:T(8,128)S(1)} all-to-all(f32[4,64,512]{2,1,0:T(8,128)S(1)} %get-tuple-element.66), channel_id=1, replica_groups=mesh['sub'=128,'split'=4] {'split'}, dimensions={0} | all-to-all | bytes 1048576 | tf_op jit(solution)/shard_map/all_to_all | solution.py:344
  130.9 17.3 %all_to_all.62 = f32[128,2,128]{2,1,0:T(2,128)S(1)} all-to-all(f32[128,2,128]{2,1,0:T(2,128)S(1)} %bitcast.38), channel_id=1, replica_groups=mesh['sub'=128,'split'=4] {'sub'}, dimensions={0} | all-to-all | bytes 262144 | tf_op jit(solution)/shard_map/all_to_all | solution.py:369
  148.2 1.0 step_6.1
  149.2 12.4 %all_to_all.63.refs_9_ = f32[4,64,512]{2,1,0:T(8,128)S(1)} all-to-all(f32[4,64,512]{2,1,0:T(8,128)S(1)} %get-tuple-element.72), channel_id=1, replica_groups=mesh['sub'=128,'split'=4] {'split'}, dimensions={0} | all-to-all | bytes 1048576 | tf_op jit(solution)/shard_map/all_to_all | solution.py:344
  161.6 0.8 step_7.1
  162.4 11.6 %all_to_all.64.refs_0_ = f32[4,64,512]{2,1,0:T(8,128)S(1)} all-to-all(f32[4,64,512]{2,1,0:T(8,128)S(1)} %get-tuple-element.75), channel_id=1, replica_groups=mesh['sub'=128,'split'=4] {'split'}, dimensions={0} | all-to-all | bytes 1048576 | tf_op jit(solution)/shard_map/all_to_all | solution.py:344
  174.0 0.9 last.1
  (17 shorter events, 0.5 us)
Async XLA Ops:
  0.6 9.5 %copy-start.7 = (s32[1,128]{1,0:T(1,128)S(1)}, s32[1,128]{1,0:T(1,128)}, u32[]{:S(2)}) copy-start(s32[1,128]{1,0:T(1,128)} %refs_1_.7) | copy-start | bytes 1540
  5.9 13.8 %all-to-all-start = ((f32[4,64,512]{2,1,0:T(8,128)}), f32[4,64,512]{2,1,0:T(8,128)S(1)}, u32[]{:S(2)}, u32[]{:S(2)}) async-start(f32[4,64,512]{2,1,0:T(8,128)} %get-tuple-element.47), calls=%async_computation | async-start | bytes 1048576 | tf_op jit(solution)/shard_map/all_to_all | solution.py:344
  10.2 9.5 %copy-start.2 = (s32[1,64,128]{2,1,0:T(8,128)S(1)}, s32[1,64,128]{2,1,0:T(8,128)}, u32[]{:S(2)}) copy-start(s32[1,64,128]{2,1,0:T(8,128)} %param.19) | copy-start | bytes 98308
  10.2 9.5 %copy-start.3 = (f32[1,64,128]{2,1,0:T(8,128)S(1)}, f32[1,64,128]{2,1,0:T(8,128)}, u32[]{:S(2)}) copy-start(f32[1,64,128]{2,1,0:T(8,128)} %param.16) | copy-start | bytes 98308
  10.2 9.5 %copy-start.5 = (s32[1,128]{1,0:T(1,128)S(1)}, s32[1,128]{1,0:T(1,128)}, u32[]{:S(2)}) copy-start(s32[1,128]{1,0:T(1,128)} %refs_5_.15) | copy-start | bytes 1540
  10.2 9.5 %copy-start.6 = (f32[1,128]{1,0:T(1,128)S(1)}, f32[1,128]{1,0:T(1,128)}, u32[]{:S(2)}) copy-start(f32[1,128]{1,0:T(1,128)} %refs_1_.11) | copy-start | bytes 1540
  19.7 1.4 copy-start
  21.9 39.4 %copy-start.1 = (bf16[3,512,512]{2,1,0:T(8,128)(2,1)S(1)}, bf16[3,512,512]{2,1,0:T(8,128)(2,1)}, u32[]{:S(2)}) copy-start(bf16[3,512,512]{2,1,0:T(8,128)(2,1)} %get-tuple-element.43.refs_1_) | copy-start | bytes 4718596
  161.6 12.4 %copy-start.4 = (bf16[512,512]{1,0:T(8,128)(2,1)S(1)}, bf16[512,512]{1,0:T(8,128)(2,1)}, u32[]{:S(2)}) copy-start(bf16[512,512]{1,0:T(8,128)(2,1)} %get-tuple-element.77.refs_4_) | copy-start | bytes 1572868

commit v2 on v1

--- a/solution.py
+++ b/solution.py
@@ -10,7 +10,6 @@
 DMAX = 5
 STRIDE = 4
 PARTS = 4
-NEAR = 1
 
 angular = 0.7
 
@@ -54,10 +53,10 @@
     return lax.broadcasted_iota(jnp.int32, shape, dim)
 
 
-def start_strips(matrix, strips, sems, forward=True):
+def start_strips(matrix, strips, sems):
     copies = {}
     width = strips.shape[2]
-    for part in range(PARTS) if forward else reversed(range(PARTS)):
+    for part in range(PARTS):
         rows = pl.ds(part * strips.shape[1] // PARTS, strips.shape[1] // PARTS)
         for strip in range(strips.shape[0]):
             copies[part, strip] = pltpu.make_async_copy(
@@ -69,18 +68,17 @@
     return copies
 
 
-def part_rows(strips, copies, part):
-    count, rows, width = strips.shape
-    nodes = rows // PARTS
+def strip_rows(strips, part, strip):
+    nodes = strips.shape[1] // PARTS
     ports = nodes // STRIDE
-    columns = []
-    for strip in range(count):
-        copies[part, strip].wait()
-        pieces = [
-            strips[strip, pl.ds(part * nodes + lane, ports, stride=STRIDE), :] for lane in range(STRIDE)
-        ]
-        columns.append(jnp.concatenate(pieces, 0))
-    return jnp.concatenate(columns, 1)
+    pieces = [strips[strip, pl.ds(part * nodes + lane, ports, stride=STRIDE), :] for lane in range(STRIDE)]
+    return jnp.concatenate(pieces, 0)
+
+
+def port_first(size):
+    node = iota((1, size), 1)
+    new = (node % STRIDE) * (size // STRIDE) + node // STRIDE
+    return (iota((size, size), 0) == new).astype(F32).astype(BF16)
 
 
 def product(stacked, cont, high, low, dims):
@@ -89,66 +87,49 @@
     return both[:cont] + both[cont:] + rest
 
 
-def first_body(*refs):
-    ins, (matrix, table, out, *held, small_sems, strips, sems, block, sent) = refs[:7], refs[7:]
+def first_body(capacity, count, *refs):
+    ins, refs = refs[: count + 1], refs[count + 1 :]
+    matrix = ins[-1]
+    table, target, order, high, low, out, *held = refs
+    *held, small_sems, strips, sems = held
     fetches = [pltpu.make_async_copy(a, b, small_sems.at[n]) for n, (a, b) in enumerate(zip(ins, held))]
     for copy in fetches:
         copy.start()
     copies = start_strips(matrix, strips, sems)
+    cont, nodes = held[3].shape
+    ports = nodes // STRIDE
+    moved = port_first(nodes)
+    order[...] = moved
+    width = 2 * ports
+    moved = port_first(width)
+    chunk = width // STRIDE
     for copy in fetches:
         copy.wait()
-    amp, phase, comp, volt, start, delay, opens = held
-    cont, nodes = volt.shape
-    ports = nodes // STRIDE
+    amp, phase, comp, volt, start, delay, opens, partner = held
     times = (iota((STEPS, nodes), 0) + 1).astype(F32)
     source = amp[...] * jnp.cos(angular * times + phase[...])
-    table[0:STEPS] = source
-    table[STEPS:] = jnp.broadcast_to(comp[...], (STEPS, nodes))
-    history = jnp.where(0 < delay[...], start[...], 0.0)
-    inject = jnp.where(0 < opens[...], history, 0.0)
-    place = (iota((ports, nodes), 1) == STRIDE * iota((ports, nodes), 0)).astype(F32).astype(BF16)
-    right = source[0:1] + comp[...] * volt[...] - stacked_exact_dot(inject, place, NN)
-    stacked = jnp.concatenate(two_pieces(right), 0)
-    leaving = []
-    for part in range(PARTS):
-        high, low = two_pieces(part_rows(strips, copies, part))
-        block[part] = product(stacked, cont, high, low, NT)
-        leaving.append(pltpu.make_async_copy(block.at[part], out.at[part], sent.at[part]))
-        leaving[-1].start()
-    for copy in leaving:
-        copy.wait()
-
-
-def prepare_body(
-    capacity, table, partner, matrix, low_out, high_near, table_out, target, order_out, high_far, strips, sems, high, order, sent
-):
-    copies = start_strips(matrix, strips, sems, forward=False)
-    nodes = table.shape[1]
-    ports = nodes // STRIDE
-    new = iota((nodes, nodes), 0)
-    old = STRIDE * (new % ports) + new // ports
-    moved = (iota((nodes, nodes), 1) == old).astype(F32).astype(BF16)
-    order[...] = moved
-    leaving = [pltpu.make_async_copy(order, order_out, sent.at[PARTS - NEAR])]
-    leaving[-1].start()
-    table_out[...] = stacked_exact_dot(table[...], moved, NT)
+    given = jnp.concatenate([volt[...], source, jnp.broadcast_to(comp[...], (STEPS, nodes))], 0)
+    given = stacked_exact_dot(given, order[...], NT)
+    table[...] = given[cont:]
     across = jnp.broadcast_to(partner[...].astype(F32), (ports, ports))
     earlier = (across == across.T) & (iota((ports, ports), 0) < iota((ports, ports), 1))
     rank = jnp.sum(earlier.astype(F32), axis=0, keepdims=True).astype(jnp.int32)
     target[...] = partner[...] * capacity + rank
-    for part in reversed(range(PARTS)):
-        pieces = two_pieces(part_rows(strips, copies, part))
-        terms = [lax.dot_general(moved, piece, NT, preferred_element_type=F32).astype(BF16) for piece in pieces]
-        low_out[part] = terms[1]
-        if part < NEAR:
-            high_near[part] = terms[0]
-        else:
-            far = part - NEAR
-            high[far] = terms[0]
-            leaving.append(pltpu.make_async_copy(high.at[far], high_far.at[far], sent.at[far]))
-            leaving[-1].start()
-    for copy in leaving:
+    history = history_at(0, start[...], delay[...], [])
+    stacked = stacked_right(0, given[:cont], history, table, opens)
+    for copy in copies.values():
         copy.wait()
+    for part in range(PARTS):
+        for pair in range(nodes // width):
+            rows = jnp.concatenate([strip_rows(strips, part, strip) for strip in (2 * pair, 2 * pair + 1)], 1)
+            for piece, piece_out in zip(two_pieces(rows), (high, low)):
+                term = lax.dot_general(moved, piece, NT, preferred_element_type=F32).astype(BF16)
+                for lane in range(STRIDE):
+                    here = lane * ports + pair * chunk
+                    piece_out[part, here : here + chunk, :] = term[lane * chunk : (lane + 1) * chunk]
+        if part > 0:
+            out[part - 1] = product(stacked, cont, high[part - 1], low[part - 1], NN)
+    out[PARTS - 1] = product(stacked, cont, high[PARTS - 1], low[PARTS - 1], NN)
 
 
 def history_at(step, start, delay, far):
@@ -175,19 +156,21 @@
     return (iota((slots, target.shape[1]), 0) == target[...]).astype(F32).astype(BF16)
 
 
-def multiply(step, volt, history, highs, low, table, opens, out):
-    cont, nodes = volt.shape
-    ports = nodes // STRIDE
+def stacked_right(step, volt, history, table, opens):
+    ports = history.shape[1]
     right = table[step : step + 1] + table[STEPS : STEPS + 1] * volt
     inject = jnp.where(step < opens[...], history, 0.0)
     right = jnp.concatenate([right[:, :ports] - inject, right[:, ports:]], 1)
-    stacked = jnp.concatenate(two_pieces(right), 0)
+    return jnp.concatenate(two_pieces(right), 0)
+
+
+def multiply(step, volt, history, high, low, table, opens, out):
+    stacked = stacked_right(step, volt, history, table, opens)
     for part in range(PARTS):
-        high = highs[0][part] if part < NEAR else highs[1][part - NEAR]
-        out[part] = product(stacked, cont, high, low[part], NN)
-
-
-def odd_body(step, anchors, near, high, low, table, start, delay, opens, impedance, history, partial, *refs):
+        out[part] = product(stacked, volt.shape[0], high[part], low[part], NN)
+
+
+def odd_body(step, anchors, high, low, table, start, delay, opens, impedance, history, partial, *refs):
     far = [(anchor, ref[...]) for anchor, ref in zip(anchors, refs)]
     out, kept, *outgoing = refs[len(anchors) :]
     total = total_of(partial)
@@ -195,10 +178,10 @@
         ref[...] = outgoing_of(step - 1, total, impedance, history[...], opens)
     now = history_at(step, start[...], delay[...], far)
     kept[...] = now
-    multiply(step, total, now, (near, high), low, table, opens, out)
-
-
-def even_body(step, anchors, near, high, low, table, start, delay, opens, target, volt, buffer, *refs):
+    multiply(step, total, now, high, low, table, opens, out)
+
+
+def even_body(step, anchors, high, low, table, start, delay, opens, target, volt, buffer, *refs):
     out, kept, *newest = refs[len(anchors) :]
     cont, ports = start.shape
     both = exact_dot(buffer[...], onehot_of(target, buffer.shape[0]), TN)
@@ -208,7 +191,7 @@
     far = [(anchor, ref[...]) for anchor, ref in zip(anchors, refs)] + [(step - DMIN, latest[0])]
     now = history_at(step, start[...], delay[...], far)
     kept[...] = now
-    multiply(step, volt[...], now, (near, high), low, table, opens, out)
+    multiply(step, volt[...], now, high, low, table, opens, out)
 
 
 def route_body(step, partial, impedance, history, opens, target, before, volt, buffer):
@@ -227,18 +210,17 @@
     volt[...] = stacked_exact_dot(total, order[...], NN)
 
 
-def call(body, shapes, *arrays, name, far_in=(), far_out=(), scratch=()):
+def call(body, shapes, *arrays, name, away=(), scratch=()):
     whole = pl.BlockSpec(memory_space=pltpu.VMEM)
-    away = pl.BlockSpec(memory_space=pltpu.HBM)
     return pl.pallas_call(
         body,
-        in_specs=[whole] * len(arrays) + [away] * len(far_in),
-        out_specs=[whole] * len(shapes) + [away] * len(far_out),
-        out_shape=[jax.ShapeDtypeStruct(*shape) for shape in shapes] + [pltpu.HBM(*shape) for shape in far_out],
+        in_specs=[whole] * len(arrays) + [pl.BlockSpec(memory_space=pltpu.HBM)] * len(away),
+        out_specs=[whole] * len(shapes),
+        out_shape=[jax.ShapeDtypeStruct(shape, kind) for shape, kind in shapes],
         scratch_shapes=list(scratch),
         compiler_params=pltpu.CompilerParams(vmem_limit_bytes=40 << 20),
         name=name,
-    )(*arrays, *[pltpu.with_memory_space_constraint(array, pltpu.HBM) for array in far_in])
+    )(*arrays, *[pltpu.with_memory_space_constraint(array, pltpu.HBM) for array in away])
 
 
 def local(
@@ -266,39 +248,25 @@
     port_shape = ((cont, ports), F32)
     split_shape = ((PARTS, cont, nodes), F32)
 
-    order_shape = ((nodes, nodes), BF16)
-    far_matrix = ((PARTS - NEAR, nodes, nodes), BF16)
-    strips = [pltpu.VMEM((STRIDE, PARTS * nodes, ports), F32), pltpu.SemaphoreType.DMA((PARTS, STRIDE))]
-
-    inputs = [source_amp, source_phase, companion, initial_voltage[0], start, delay, opens]
-    table, partial = call(
-        first_body,
-        [((2 * STEPS, nodes), F32)],
-        far_in=[*inputs, matrix],
-        far_out=[split_shape],
+    inputs = [source_amp, source_phase, companion, initial_voltage[0], start, delay, opens, partner_sub]
+    table, target, order, high, low, partial = call(
+        lambda *refs: first_body(capacity, len(inputs), *refs),
+        [
+            ((2 * STEPS, nodes), F32),
+            ((1, ports), jnp.int32),
+            ((nodes, nodes), BF16),
+            ((PARTS, nodes, nodes), BF16),
+            ((PARTS, nodes, nodes), BF16),
+            split_shape,
+        ],
+        away=[*inputs, matrix],
         scratch=[
             *[pltpu.VMEM(array.shape, array.dtype) for array in inputs],
             pltpu.SemaphoreType.DMA((len(inputs),)),
-            *strips,
-            pltpu.VMEM(*split_shape),
-            pltpu.SemaphoreType.DMA((PARTS,)),
+            pltpu.VMEM((STRIDE, PARTS * nodes, ports), F32),
+            pltpu.SemaphoreType.DMA((PARTS, STRIDE)),
         ],
         name="first_step",
-    )
-    low, near, table, target, order, high = call(
-        lambda *refs: prepare_body(capacity, *refs),
-        [
-            ((PARTS, nodes, nodes), BF16),
-            ((NEAR, nodes, nodes), BF16),
-            ((2 * STEPS, nodes), F32),
-            ((1, ports), jnp.int32),
-        ],
-        table,
-        partner_sub,
-        far_in=[matrix],
-        far_out=[order_shape, far_matrix],
-        scratch=[*strips, pltpu.VMEM(*far_matrix), pltpu.VMEM(*order_shape), pltpu.SemaphoreType.DMA((PARTS - NEAR + 1,))],
-        name="prepare",
     )
 
     history = start
@@ -309,7 +277,6 @@
             partial, history, *before = call(
                 lambda *refs, step=step, anchors=anchors: odd_body(step, anchors, *refs),
                 [split_shape, port_shape] + [port_shape] * (step + DMIN < STEPS),
-                near,
                 high,
                 low,
                 table,
@@ -327,7 +294,6 @@
             partial, history, *newest = call(
                 lambda *refs, step=step, anchors=anchors: even_body(step, anchors, *refs),
                 [split_shape] + [port_shape] * 3,
-                near,
                 high,
                 low,
                 table,

time: 176 us -> 173 us (0.983)
  blocking collectives: 146 us -> 160 us
  Pallas kernels: 18 us -> 12.6 us
  waiting for transfers between devices: 4.61 us -> 0 us
  starting transfers between devices: 4.3 us -> 0 us
    all_to_all x7 -> x8, blocking collectives: 82.9 us -> 96.6 us  [local(): lax.all_to_all(partial, 'split', split_axis=0, concat_axis=0, tiled=True)]
    pallas_call x13 -> x12, Pallas kernels: 18 us -> 12.6 us  [call(): pl.pallas_call(body, in_specs=[whole] * len(arrays) + [pl.BlockSpec(memor...]
    all_to_all x1 -> x0, waiting for transfers between devices: 4.61 us -> none  [local(): lax.all_to_all(partial, 'split', split_axis=0, concat_axis=0, tiled=True)]
    all_to_all x1 -> x0, starting transfers between devices: 4.3 us -> none  [local(): lax.all_to_all(partial, 'split', split_axis=0, concat_axis=0, tiled=True)]
  transfers between devices with their start and end apart: 1 -> 0, of which waited for: 1 -> 0; matrix products, arithmetic and copies ran while one was open for 0% -> 0% of each run, Pallas kernels for 3% -> 0%
where the time goes in v2:
time: 173 us
  blocking collectives  160 us (92%)
  Pallas kernels  12.6 us (7%)
    all_to_all x8, blocking collectives, local(): lax.all_to_all(partial, 'split', split_axis=0, concat_axis=0, tiled=True)  96.6 us
    all_to_all x3, blocking collectives, local(): lax.all_to_all(buffer, 'sub', split_axis=0, concat_axis=0, tiled=True)  63 us
    pallas_call x12, Pallas kernels, call(): pl.pallas_call(body, in_specs=[whole] * len(arrays) + [pl.BlockSpec(memor...  12.6 us

profile of v2, /device:TPU:16, one launch (start us, length us, event | category | flops | bytes accessed | tf_op | source)
XLA Modules:
  0.0 173.0 jit_solution(2146562460761591706)
XLA Ops:
  0.7 4.7 %first_step.1 = (f32[16,512]{1,0:T(8,128)S(1)}, s32[1,128]{1,0:T(1,128)S(1)}, bf16[512,512]{1,0:T(8,128)(2,1)S(1)}, bf16[4,512,512]{2,1,0:T(8,128)(2,1)S(1)}, bf...) custom-call(f32[1,512]{1,0:T(1,128)} %refs_0_.1, f32[1,512]{1,0:T(1,128)} %refs_1_.5, f32[1,512]{1,0:T(1,128)} %refs_2_.1, ...), custom_call_target="tpu_custom_call" | custom-call | tf_op jit(solution)/shard_map/first_step/pallas_call | solution.py:215
  5.4 13.6 %all_to_all.55.refs_8_ = f32[4,64,512]{2,1,0:T(8,128)S(1)} all-to-all(f32[4,64,512]{2,1,0:T(8,128)S(1)} %get-tuple-element.43), channel_id=1, replica_groups=mesh['sub'=128,'split'=4] {'split'}, dimensions={0} | all-to-all | bytes 1048576 | tf_op jit(solution)/shard_map/all_to_all | solution.py:310
  18.9 0.0 copy-done.2
  18.9 0.8 step_1.1
  19.8 11.0 %all_to_all.56.refs_0_ = f32[4,64,512]{2,1,0:T(8,128)S(1)} all-to-all(f32[4,64,512]{2,1,0:T(8,128)S(1)} %get-tuple-element.44), channel_id=1, replica_groups=mesh['sub'=128,'split'=4] {'split'}, dimensions={0} | all-to-all | bytes 1048576 | tf_op jit(solution)/shard_map/all_to_all | solution.py:310
  30.7 0.2 route_1.1
  31.0 28.4 %all_to_all.57 = f32[128,2,128]{2,1,0:T(2,128)S(1)} all-to-all(f32[128,2,128]{2,1,0:T(2,128)S(1)} %bitcast.36), channel_id=1, replica_groups=mesh['sub'=128,'split'=4] {'sub'}, dimensions={0} | all-to-all | bytes 262144 | tf_op jit(solution)/shard_map/all_to_all | solution.py:335
  59.3 1.0 step_2.1
  60.4 12.4 %all_to_all.58.refs_8_ = f32[4,64,512]{2,1,0:T(8,128)S(1)} all-to-all(f32[4,64,512]{2,1,0:T(8,128)S(1)} %get-tuple-element.50), channel_id=1, replica_groups=mesh['sub'=128,'split'=4] {'split'}, dimensions={0} | all-to-all | bytes 1048576 | tf_op jit(solution)/shard_map/all_to_all | solution.py:310
  72.8 0.8 step_3.1
  73.6 11.6 %all_to_all.59.refs_0_ = f32[4,64,512]{2,1,0:T(8,128)S(1)} all-to-all(f32[4,64,512]{2,1,0:T(8,128)S(1)} %get-tuple-element.53), channel_id=1, replica_groups=mesh['sub'=128,'split'=4] {'split'}, dimensions={0} | all-to-all | bytes 1048576 | tf_op jit(solution)/shard_map/all_to_all | solution.py:310
  85.2 0.2 route_3.1
  85.4 17.3 %all_to_all.60 = f32[128,2,128]{2,1,0:T(2,128)S(1)} all-to-all(f32[128,2,128]{2,1,0:T(2,128)S(1)} %bitcast.37), channel_id=1, replica_groups=mesh['sub'=128,'split'=4] {'sub'}, dimensions={0} | all-to-all | bytes 262144 | tf_op jit(solution)/shard_map/all_to_all | solution.py:335
  102.7 1.0 step_4.1
  103.7 12.4 %all_to_all.61.refs_8_ = f32[4,64,512]{2,1,0:T(8,128)S(1)} all-to-all(f32[4,64,512]{2,1,0:T(8,128)S(1)} %get-tuple-element.59), channel_id=1, replica_groups=mesh['sub'=128,'split'=4] {'split'}, dimensions={0} | all-to-all | bytes 1048576 | tf_op jit(solution)/shard_map/all_to_all | solution.py:310
  116.2 0.8 step_5.1
  117.0 11.6 %all_to_all.62.refs_0_ = f32[4,64,512]{2,1,0:T(8,128)S(1)} all-to-all(f32[4,64,512]{2,1,0:T(8,128)S(1)} %get-tuple-element.62), channel_id=1, replica_groups=mesh['sub'=128,'split'=4] {'split'}, dimensions={0} | all-to-all | bytes 1048576 | tf_op jit(solution)/shard_map/all_to_all | solution.py:310
  128.6 0.2 route_5.1
  128.8 17.3 %all_to_all.63 = f32[128,2,128]{2,1,0:T(2,128)S(1)} all-to-all(f32[128,2,128]{2,1,0:T(2,128)S(1)} %bitcast.38), channel_id=1, replica_groups=mesh['sub'=128,'split'=4] {'sub'}, dimensions={0} | all-to-all | bytes 262144 | tf_op jit(solution)/shard_map/all_to_all | solution.py:335
  146.1 1.0 step_6.1
  147.2 12.4 %all_to_all.64.refs_8_ = f32[4,64,512]{2,1,0:T(8,128)S(1)} all-to-all(f32[4,64,512]{2,1,0:T(8,128)S(1)} %get-tuple-element.68), channel_id=1, replica_groups=mesh['sub'=128,'split'=4] {'split'}, dimensions={0} | all-to-all | bytes 1048576 | tf_op jit(solution)/shard_map/all_to_all | solution.py:310
  159.6 0.8 step_7.1
  160.4 11.6 %all_to_all.65.refs_0_ = f32[4,64,512]{2,1,0:T(8,128)S(1)} all-to-all(f32[4,64,512]{2,1,0:T(8,128)S(1)} %get-tuple-element.71), channel_id=1, replica_groups=mesh['sub'=128,'split'=4] {'split'}, dimensions={0} | all-to-all | bytes 1048576 | tf_op jit(solution)/shard_map/all_to_all | solution.py:310
  172.0 0.9 last.1
  (7 shorter events, 0.0 us)
Async XLA Ops:
  0.6 18.3 %copy-start = (s32[1,64,128]{2,1,0:T(8,128)S(1)}, s32[1,64,128]{2,1,0:T(8,128)}, u32[]{:S(2)}) copy-start(s32[1,64,128]{2,1,0:T(8,128)} %param.19) | copy-start | bytes 98308
  0.6 18.3 %copy-start.1 = (f32[1,64,128]{2,1,0:T(8,128)S(1)}, f32[1,64,128]{2,1,0:T(8,128)}, u32[]{:S(2)}) copy-start(f32[1,64,128]{2,1,0:T(8,128)} %param.16) | copy-start | bytes 98308
  0.7 18.3 %copy-start.2 = (f32[1,128]{1,0:T(1,128)S(1)}, f32[1,128]{1,0:T(1,128)}, u32[]{:S(2)}) copy-start(f32[1,128]{1,0:T(1,128)} %refs_1_.9) | copy-start | bytes 1540
  0.7 18.3 %copy-start.3 = (s32[1,128]{1,0:T(1,128)S(1)}, s32[1,128]{1,0:T(1,128)}, u32[]{:S(2)}) copy-start(s32[1,128]{1,0:T(1,128)} %refs_4_.13) | copy-start | bytes 1540

commit v3 on v2

--- a/solution.py
+++ b/solution.py
@@ -54,17 +54,12 @@
 
 
 def start_strips(matrix, strips, sems):
-    copies = {}
+    copies = []
     width = strips.shape[2]
-    for part in range(PARTS):
-        rows = pl.ds(part * strips.shape[1] // PARTS, strips.shape[1] // PARTS)
-        for strip in range(strips.shape[0]):
-            copies[part, strip] = pltpu.make_async_copy(
-                matrix.at[rows, pl.ds(strip * width, width)],
-                strips.at[strip, rows, :],
-                sems.at[part, strip],
-            )
-            copies[part, strip].start()
+    for strip in range(strips.shape[0]):
+        columns = matrix.at[:, pl.ds(strip * width, width)]
+        copies.append(pltpu.make_async_copy(columns, strips.at[strip], sems.at[strip]))
+        copies[-1].start()
     return copies
 
 
@@ -93,9 +88,9 @@
     table, target, order, high, low, out, *held = refs
     *held, small_sems, strips, sems = held
     fetches = [pltpu.make_async_copy(a, b, small_sems.at[n]) for n, (a, b) in enumerate(zip(ins, held))]
+    copies = start_strips(matrix, strips, sems)
     for copy in fetches:
         copy.start()
-    copies = start_strips(matrix, strips, sems)
     cont, nodes = held[3].shape
     ports = nodes // STRIDE
     moved = port_first(nodes)
@@ -117,7 +112,7 @@
     target[...] = partner[...] * capacity + rank
     history = history_at(0, start[...], delay[...], [])
     stacked = stacked_right(0, given[:cont], history, table, opens)
-    for copy in copies.values():
+    for copy in copies:
         copy.wait()
     for part in range(PARTS):
         for pair in range(nodes // width):
@@ -166,8 +161,11 @@
 
 def multiply(step, volt, history, high, low, table, opens, out):
     stacked = stacked_right(step, volt, history, table, opens)
+    cont = volt.shape[0]
+    rest = [jnp.dot(stacked[:cont], low[part], preferred_element_type=F32) for part in range(PARTS)]
     for part in range(PARTS):
-        out[part] = product(stacked, volt.shape[0], high[part], low[part], NN)
+        both = jnp.dot(stacked, high[part], preferred_element_type=F32)
+        out[part] = both[:cont] + both[cont:] + rest[part]
 
 
 def odd_body(step, anchors, high, low, table, start, delay, opens, impedance, history, partial, *refs):
@@ -183,7 +181,13 @@
 
 def even_body(step, anchors, high, low, table, start, delay, opens, target, volt, buffer, *refs):
     out, kept, *newest = refs[len(anchors) :]
-    cont, ports = start.shape
+    cont, nodes = volt.shape
+    half = nodes // 2
+    right = table[step : step + 1] + table[STEPS : STEPS + 1] * volt[...]
+    stacked = jnp.concatenate(two_pieces(right[:, half:]), 0)
+    for part in range(PARTS):
+        out[part] = product(stacked, cont, high[part, half:], low[part, half:], NN)
+    ports = start.shape[1]
     both = exact_dot(buffer[...], onehot_of(target, buffer.shape[0]), TN)
     latest = [both[:cont], both[cont:]]
     for ref, array in zip(newest, latest):
@@ -191,7 +195,11 @@
     far = [(anchor, ref[...]) for anchor, ref in zip(anchors, refs)] + [(step - DMIN, latest[0])]
     now = history_at(step, start[...], delay[...], far)
     kept[...] = now
-    multiply(step, volt[...], now, high, low, table, opens, out)
+    inject = jnp.where(step < opens[...], now, 0.0)
+    lower = jnp.concatenate([right[:, :ports] - inject, right[:, ports:half]], 1)
+    stacked = jnp.concatenate(two_pieces(lower), 0)
+    for part in range(PARTS):
+        out[part] += product(stacked, cont, high[part, :half], low[part, :half], NN)
 
 
 def route_body(step, partial, impedance, history, opens, target, before, volt, buffer):
@@ -264,7 +272,7 @@
             *[pltpu.VMEM(array.shape, array.dtype) for array in inputs],
             pltpu.SemaphoreType.DMA((len(inputs),)),
             pltpu.VMEM((STRIDE, PARTS * nodes, ports), F32),
-            pltpu.SemaphoreType.DMA((PARTS, STRIDE)),
+            pltpu.SemaphoreType.DMA((STRIDE,)),
         ],
         name="first_step",
     )

time: 173 us -> 173 us (level)
  no operation moved by 1% of the time
where the time goes in v3:
time: 173 us
  blocking collectives  160 us (92%)
  Pallas kernels  12.3 us (7%)
    all_to_all x8, blocking collectives, local(): lax.all_to_all(partial, 'split', split_axis=0, concat_axis=0, tiled=True)  96.6 us
    all_to_all x3, blocking collectives, local(): lax.all_to_all(buffer, 'sub', split_axis=0, concat_axis=0, tiled=True)  62.9 us
    pallas_call x12, Pallas kernels, call(): pl.pallas_call(body, in_specs=[whole] * len(arrays) + [pl.BlockSpec(memor...  12.3 us

profile of v3, /device:TPU:16, one launch (start us, length us, event | category | flops | bytes accessed | tf_op | source)
XLA Modules:
  0.0 172.6 jit_solution(9208814273897295605)
XLA Ops:
  0.7 4.7 %first_step.1 = (f32[16,512]{1,0:T(8,128)S(1)}, s32[1,128]{1,0:T(1,128)S(1)}, bf16[512,512]{1,0:T(8,128)(2,1)S(1)}, bf16[4,512,512]{2,1,0:T(8,128)(2,1)S(1)}, bf...) custom-call(f32[1,512]{1,0:T(1,128)} %refs_0_.1, f32[1,512]{1,0:T(1,128)} %refs_1_.5, f32[1,512]{1,0:T(1,128)} %refs_2_.1, ...), custom_call_target="tpu_custom_call" | custom-call | tf_op jit(solution)/shard_map/first_step/pallas_call | solution.py:223
  5.3 13.6 %all_to_all.55.refs_8_ = f32[4,64,512]{2,1,0:T(8,128)S(1)} all-to-all(f32[4,64,512]{2,1,0:T(8,128)S(1)} %get-tuple-element.43), channel_id=1, replica_groups=mesh['sub'=128,'split'=4] {'split'}, dimensions={0} | all-to-all | bytes 1048576 | tf_op jit(solution)/shard_map/all_to_all | solution.py:318
  18.9 0.0 copy-done
  18.9 0.8 step_1.1
  19.7 11.0 %all_to_all.56.refs_0_ = f32[4,64,512]{2,1,0:T(8,128)S(1)} all-to-all(f32[4,64,512]{2,1,0:T(8,128)S(1)} %get-tuple-element.44), channel_id=1, replica_groups=mesh['sub'=128,'split'=4] {'split'}, dimensions={0} | all-to-all | bytes 1048576 | tf_op jit(solution)/shard_map/all_to_all | solution.py:318
  30.7 0.2 route_1.1
  30.9 28.4 %all_to_all.57 = f32[128,2,128]{2,1,0:T(2,128)S(1)} all-to-all(f32[128,2,128]{2,1,0:T(2,128)S(1)} %bitcast.36), channel_id=1, replica_groups=mesh['sub'=128,'split'=4] {'sub'}, dimensions={0} | all-to-all | bytes 262144 | tf_op jit(solution)/shard_map/all_to_all | solution.py:343
  59.3 0.9 step_2.1
  60.3 12.4 %all_to_all.58.refs_8_ = f32[4,64,512]{2,1,0:T(8,128)S(1)} all-to-all(f32[4,64,512]{2,1,0:T(8,128)S(1)} %get-tuple-element.50), channel_id=1, replica_groups=mesh['sub'=128,'split'=4] {'split'}, dimensions={0} | all-to-all | bytes 1048576 | tf_op jit(solution)/shard_map/all_to_all | solution.py:318
  72.7 0.8 step_3.1
  73.5 11.6 %all_to_all.59.refs_0_ = f32[4,64,512]{2,1,0:T(8,128)S(1)} all-to-all(f32[4,64,512]{2,1,0:T(8,128)S(1)} %get-tuple-element.53), channel_id=1, replica_groups=mesh['sub'=128,'split'=4] {'split'}, dimensions={0} | all-to-all | bytes 1048576 | tf_op jit(solution)/shard_map/all_to_all | solution.py:318
  85.1 0.2 route_3.1
  85.3 17.3 %all_to_all.60 = f32[128,2,128]{2,1,0:T(2,128)S(1)} all-to-all(f32[128,2,128]{2,1,0:T(2,128)S(1)} %bitcast.37), channel_id=1, replica_groups=mesh['sub'=128,'split'=4] {'sub'}, dimensions={0} | all-to-all | bytes 262144 | tf_op jit(solution)/shard_map/all_to_all | solution.py:343
  102.6 1.0 step_4.1
  103.5 12.4 %all_to_all.61.refs_8_ = f32[4,64,512]{2,1,0:T(8,128)S(1)} all-to-all(f32[4,64,512]{2,1,0:T(8,128)S(1)} %get-tuple-element.59), channel_id=1, replica_groups=mesh['sub'=128,'split'=4] {'split'}, dimensions={0} | all-to-all | bytes 1048576 | tf_op jit(solution)/shard_map/all_to_all | solution.py:318
  116.0 0.8 step_5.1
  116.8 11.6 %all_to_all.62.refs_0_ = f32[4,64,512]{2,1,0:T(8,128)S(1)} all-to-all(f32[4,64,512]{2,1,0:T(8,128)S(1)} %get-tuple-element.62), channel_id=1, replica_groups=mesh['sub'=128,'split'=4] {'split'}, dimensions={0} | all-to-all | bytes 1048576 | tf_op jit(solution)/shard_map/all_to_all | solution.py:318
  128.4 0.2 route_5.1
  128.6 17.3 %all_to_all.63 = f32[128,2,128]{2,1,0:T(2,128)S(1)} all-to-all(f32[128,2,128]{2,1,0:T(2,128)S(1)} %bitcast.38), channel_id=1, replica_groups=mesh['sub'=128,'split'=4] {'sub'}, dimensions={0} | all-to-all | bytes 262144 | tf_op jit(solution)/shard_map/all_to_all | solution.py:343
  145.9 1.0 step_6.1
  146.8 12.4 %all_to_all.64.refs_8_ = f32[4,64,512]{2,1,0:T(8,128)S(1)} all-to-all(f32[4,64,512]{2,1,0:T(8,128)S(1)} %get-tuple-element.68), channel_id=1, replica_groups=mesh['sub'=128,'split'=4] {'split'}, dimensions={0} | all-to-all | bytes 1048576 | tf_op jit(solution)/shard_map/all_to_all | solution.py:318
  159.3 0.8 step_7.1
  160.1 11.6 %all_to_all.65.refs_0_ = f32[4,64,512]{2,1,0:T(8,128)S(1)} all-to-all(f32[4,64,512]{2,1,0:T(8,128)S(1)} %get-tuple-element.71), channel_id=1, replica_groups=mesh['sub'=128,'split'=4] {'split'}, dimensions={0} | all-to-all | bytes 1048576 | tf_op jit(solution)/shard_map/all_to_all | solution.py:318
  171.7 0.9 last.1
  (7 shorter events, 0.0 us)
Async XLA Ops:
  0.6 18.3 %copy-start = (s32[1,64,128]{2,1,0:T(8,128)S(1)}, s32[1,64,128]{2,1,0:T(8,128)}, u32[]{:S(2)}) copy-start(s32[1,64,128]{2,1,0:T(8,128)} %param.19) | copy-start | bytes 98308
  0.6 18.3 %copy-start.1 = (f32[1,64,128]{2,1,0:T(8,128)S(1)}, f32[1,64,128]{2,1,0:T(8,128)}, u32[]{:S(2)}) copy-start(f32[1,64,128]{2,1,0:T(8,128)} %param.16) | copy-start | bytes 98308
  0.7 18.3 %copy-start.2 = (f32[1,128]{1,0:T(1,128)S(1)}, f32[1,128]{1,0:T(1,128)}, u32[]{:S(2)}) copy-start(f32[1,128]{1,0:T(1,128)} %refs_1_.9) | copy-start | bytes 1540
  0.7 18.3 %copy-start.3 = (s32[1,128]{1,0:T(1,128)S(1)}, s32[1,128]{1,0:T(1,128)}, u32[]{:S(2)}) copy-start(s32[1,128]{1,0:T(1,128)} %refs_4_.13) | copy-start | bytes 1540
